TPU v7x, 256 devices: a whole 4x4x8 slice. The times are simulated.
256 devices in a mesh: seq: 64 (over z, y, core), tp: 4 (over x).
Axes of the slice: x: 4, y: 4, z: 8, core: 2. Of those that a mesh axis runs over, the one named last changes fastest.
Arguments:
- normed: bfloat16 [32768, 2048], P('seq', 'tp'), may hold values from -24 to 24
- cluster: int32 [32768, 1], P('seq'), may hold values from 0 to 127; in each aligned block of 512 rows (0 to 511, 512 to 1023, ...) at most 8 rows name the same one
- w_query: bfloat16 [2048, 2048], P(None, 'tp'), may hold values from -1 to 1
- w_key: bfloat16 [2048, 2048], P(None, 'tp'), may hold values from -1 to 1
- w_value: bfloat16 [2048, 2048], P(None, 'tp'), may hold values from -0.125 to 0.125
- w_out: bfloat16 [2048, 2048], P('tp'), may hold values from -0.125 to 0.125
- grad_out: bfloat16 [32768, 2048], P('seq', 'tp'), may hold values from -6 to 6
Outputs:
- attended: bfloat16 [32768, 2048], P('seq', 'tp')
- grad_normed: float32 [32768, 2048], P('seq', 'tp')
Inputs may be any that keep to these rules, and one draw needn't show every extreme that they name: Among the tokens of one index of seq no cluster id appears more than 8 times, and some id appears exactly 8 times; every id appears somewhere.
All inputs are finite; a program needn't handle non-finite values.
Results may differ from a plain program's by a relative error of at most 0.011.
The roundings to bfloat16 on the way count: a program that leaves them out, or rounds other values in their place, can miss the bound.
Values may be sent and summed in bfloat16 or wider, within the bound.
A program may use at most 128 MiB of HBM per device.

v0:
```python
import jax
import jax.numpy as jnp
from jax import lax
from jax.sharding import PartitionSpec as P

HEAD_DIM = 128
CLUSTERS = 128
CAP = 256
MOST = 8


def entering(x, axis, combine, identity):
    count, position = (lax.axis_size(axis), lax.axis_index(axis))
    everything = lax.all_gather(x, axis)
    start = jnp.broadcast_to(jnp.asarray(identity, x.dtype), x.shape)

    def lap(k, before):
        reached = k < position
        new = combine(before, everything[k])
        return jnp.where(reached, new, before)

    return lax.fori_loop(0, count, lap, start)


def cluster_probs(query, key_rows, usable):
    score_scale = query.shape[-1] ** (-0.5)
    scores = (
        jnp.einsum("qhd,khd->hqk", query, key_rows, preferred_element_type=jnp.float32)
        * score_scale
    )
    scores = jnp.where(usable[None, None, :], scores, -1e30)
    row_top = jnp.max(scores, axis=-1, keepdims=True)
    raised = jnp.exp(scores - row_top)
    return raised / jnp.sum(raised, axis=-1, keepdims=True)


def unpack(packed):
    width = packed.shape[1] // 3
    rows = packed.shape[0]
    query = packed[:, :width].reshape(rows, -1, HEAD_DIM)
    key_rows = packed[:, width : 2 * width].reshape(rows, -1, HEAD_DIM)
    value_rows = packed[:, 2 * width :].reshape(rows, -1, HEAD_DIM)
    return (query, key_rows, value_rows)


def forward_one(packed, usable):
    query, key_rows, value_rows = unpack(packed)
    probs = cluster_probs(query, key_rows, usable)
    mixed = jnp.einsum(
        "hqk,khd->qhd", probs.astype(jnp.bfloat16), value_rows, preferred_element_type=jnp.float32
    )
    return mixed.reshape(packed.shape[0], -1).astype(jnp.bfloat16)


def attention_core(packed, usable, grad_rows):
    query, key_rows, value_rows = unpack(packed)
    rows = packed.shape[0]
    score_scale = query.shape[-1] ** (-0.5)
    grad_heads = grad_rows.reshape(rows, -1, HEAD_DIM)
    probs = cluster_probs(query, key_rows, usable)
    rounded = probs.astype(jnp.bfloat16)
    mixed = jnp.einsum("hqk,khd->qhd", rounded, value_rows, preferred_element_type=jnp.float32)
    grad_value = jnp.einsum("hqk,qhd->khd", rounded, grad_heads, preferred_element_type=jnp.float32)
    grad_probs = jnp.einsum(
        "qhd,khd->hqk", grad_heads, value_rows, preferred_element_type=jnp.float32
    )
    inner = jnp.sum(grad_probs * probs, axis=-1, keepdims=True)
    grad_scores = (probs * (grad_probs - inner) * score_scale).astype(jnp.bfloat16)
    grad_query = jnp.einsum(
        "hqk,khd->qhd", grad_scores, key_rows, preferred_element_type=jnp.float32
    )
    grad_key = jnp.einsum("hqk,qhd->khd", grad_scores, query, preferred_element_type=jnp.float32)
    grads = jnp.concatenate(
        [
            grad_query.reshape(rows, -1).astype(jnp.bfloat16),
            grad_key.reshape(rows, -1).astype(jnp.bfloat16),
            grad_value.reshape(rows, -1).astype(jnp.bfloat16),
        ],
        axis=1,
    )
    return (mixed.reshape(rows, -1).astype(jnp.bfloat16), grads)


def body(normed, cluster, w_query, w_key, w_value, w_out, grad_out):
    seq_count = lax.axis_size("seq")
    local_cols = w_query.shape[1]
    cluster_here = CLUSTERS // seq_count
    cluster_ids = cluster[:, 0]
    columns = jnp.arange(CLUSTERS, dtype=jnp.int32)
    one_hot = (cluster_ids[:, None] == columns[None, :]).astype(jnp.int32)
    running = jnp.cumsum(one_hot, axis=0)
    local_rank = jnp.sum((running - one_hot) * one_hot, axis=1)
    counts = running[-1]
    offsets = entering(
        counts, "seq", lambda earlier, later: earlier + later, jnp.zeros_like(counts)
    )
    global_rank = local_rank + jnp.sum(one_hot * offsets[None, :], axis=1)
    kept_rows = (global_rank < CAP).astype(jnp.bfloat16)
    slot_index = cluster_ids * MOST + local_rank
    piece = lax.all_gather(normed, "tp", axis=1, tiled=True)
    query_sum = jnp.dot(piece, w_query, preferred_element_type=jnp.float32)
    key_sum = jnp.dot(piece, w_key, preferred_element_type=jnp.float32)
    value_sum = jnp.dot(piece, w_value, preferred_element_type=jnp.float32)
    packed_rows = jnp.concatenate(
        [
            query_sum.astype(jnp.bfloat16),
            key_sum.astype(jnp.bfloat16),
            value_sum.astype(jnp.bfloat16),
        ],
        axis=1,
    )
    head_grads = (
        lax.dot_general(
            lax.all_gather(grad_out, "tp", axis=1, tiled=True),
            w_out,
            (((1,), (1,)), ((), ())),
            preferred_element_type=jnp.float32,
        ).astype(jnp.bfloat16)
        * kept_rows[:, None]
    )

    def to_owners(rows):
        buffer = jnp.zeros((CLUSTERS * MOST, rows.shape[1]), rows.dtype).at[slot_index].set(rows)
        return buffer.reshape(seq_count, cluster_here, MOST, rows.shape[1])

    flags = (
        jnp.zeros((CLUSTERS * MOST,), jnp.bfloat16)
        .at[slot_index]
        .set(kept_rows)
        .reshape(seq_count, cluster_here, MOST)
    )

    def from_owners(slots):
        return slots.reshape(cluster_here, seq_count, MOST, slots.shape[-1])

    def to_tokens(returned):
        return (
            returned.reshape(CLUSTERS * MOST, returned.shape[-1])[slot_index] * kept_rows[:, None]
        )

    arrived, arrived_flags = (
        lax.all_to_all(to_owners(packed_rows), "seq", split_axis=0, concat_axis=2, tiled=True),
        lax.all_to_all(flags, "seq", split_axis=0, concat_axis=2, tiled=True),
    )
    usable = arrived_flags[0] > 0
    mixed_slots = lax.map(lambda pair: forward_one(pair[0], pair[1]), (arrived[0], usable))
    heads_tok = to_tokens(
        lax.all_to_all(from_owners(mixed_slots), "seq", split_axis=1, concat_axis=0, tiled=True)
    )
    grad_arrived = lax.all_to_all(
        to_owners(head_grads), "seq", split_axis=0, concat_axis=2, tiled=True
    )
    grad_slots = lax.map(
        lambda triple: attention_core(triple[0], triple[1], triple[2])[1],
        (arrived[0], usable, grad_arrived[0]),
    )
    grads_tok = to_tokens(
        lax.all_to_all(from_owners(grad_slots), "seq", split_axis=1, concat_axis=0, tiled=True)
    )
    partial_out = jnp.dot(heads_tok, w_out, preferred_element_type=jnp.float32)
    attended = lax.psum_scatter(partial_out, "tp", scatter_dimension=1, tiled=True).astype(
        jnp.bfloat16
    )
    contract = (((1,), (1,)), ((), ()))
    partial_grad = lax.dot_general(
        grads_tok[:, :local_cols], w_query, contract, preferred_element_type=jnp.float32
    )
    partial_grad = partial_grad + lax.dot_general(
        grads_tok[:, local_cols : 2 * local_cols],
        w_key,
        contract,
        preferred_element_type=jnp.float32,
    )
    partial_grad = partial_grad + lax.dot_general(
        grads_tok[:, 2 * local_cols :], w_value, contract, preferred_element_type=jnp.float32
    )
    grad_normed = lax.psum_scatter(partial_grad, "tp", scatter_dimension=1, tiled=True)
    return (attended, grad_normed)


def solution(mesh):
    in_specs = (
        P("seq", "tp"),
        P("seq", None),
        P(None, "tp"),
        P(None, "tp"),
        P(None, "tp"),
        P("tp", None),
        P("seq", "tp"),
    )
    out_specs = (P("seq", "tp"), P("seq", "tp"))
    return jax.shard_map(body, mesh=mesh, in_specs=in_specs, out_specs=out_specs, check_vma=False)
```

profile of v0, /device:TPU:1, one launch (start us, length us, event | category | flops | bytes accessed | tf_op | source)
XLA Modules:
  0.0 460.2 jit_solution(15803309775498486307)
XLA Ops:
  7.9 0.8 copy.71
  9.0 44.2 %all-gather = s32[64,1,128]{2,1,0:T(1,128)S(1)} all-gather(s32[1,1,128]{2,1,0:T(1,128)S(1)} %slice_bitcast_fusion.1), channel_id=1, replica_groups=mesh['seq'=64,'tp'=4] {'seq'}, dimensions={0}, use_global_device_ids=true | all-gather | bytes 33280 | tf_op jit(solution)/shard_map/all_gather | solution.py:14
  53.3 2.6 while.36
  55.9 1.0 select_reduce_fusion
  57.5 3.8 scatter_custom_fusion.1
  61.3 0.7 reshape.110
  62.0 6.8 %all-to-all-start.1 = ((bf16[64,2,8]{2,1,0:T(2,128)(2,1)}), bf16[64,2,8]{2,1,0:T(2,128)(2,1)S(1)}, u32[]{:S(2)}, u32[]{:S(2)}) async-start(bf16[64,2,8]{2,1,0:T(2,128)(2,1)} %reshape.110), calls=%async_computation.1 | async-start | bytes 65536 | tf_op jit(solution)/shard_map/all_to_all | solution.py:143
  68.9 3.7 convolution_convert_fusion.1
  72.6 1.3 convolution_convert_fusion.2
  74.2 1.3 convolution_convert_fusion.3
  75.5 1.2 pad_maximum_fusion
  76.8 2.6 copy.73
  79.4 6.0 %scatter_custom_fusion = bf16[1024,1536]{1,0:T(8,128)(2,1)} fusion(s32[512]{0:T(512)S(1)} %bitcast.181, bf16[512,1536]{1,0:T(8,128)(2,1)} %copy.73, bf16[]{:T(256)} %constant.82.clone.1), kind=kCustom, calls=%fused_computation.59 | custom fusion | bytes 3146240 | tf_op jit(solution)/shard_map/scatter | solution.py:123
  85.4 10.5 %all-to-all-start = ((bf16[64,2,8,1536]{3,2,1,0:T(8,128)(2,1)}), bf16[64,2,8,1536]{3,2,1,0:T(8,128)(2,1)}, u32[]{:S(2)}, u32[]{:S(2)}) async-start(bf16[64,2,8,1536]{3,2,1,0:T(8,128)(2,1)} %bitcast.169), calls=%async_computation | async-start | bytes 6291456 | tf_op jit(solution)/shard_map/all_to_all | solution.py:142
  96.8 36.0 %all-gather.6.cloned.1.call-done = bf16[512,2048]{1,0:T(8,128)(2,1)} async-done(((bf16[512,512]{1,0:T(8,128)(2,1)}), bf16[512,2048]{1,0:T(8,128)(2,1)}) %all-gather.6.cloned.1.call-update) | async-done | bytes 2097168 | tf_op jit(solution)/shard_map/all_gather | solution.py:114
  132.8 2.9 fusion.49
  135.7 3.5 scatter_custom_fusion.2
  139.2 29.2 %all-to-all-done = bf16[64,2,8,1536]{3,2,1,0:T(8,128)(2,1)} async-done(((bf16[64,2,8,1536]{3,2,1,0:T(8,128)(2,1)}), bf16[64,2,8,1536]{3,2,1,0:T(8,128)(2,1)}, u32[]{:S(2)}, u32[]{:S(2)}) %all-to-all-start) | async-done | bytes 3145760 | tf_op jit(solution)/shard_map/all_to_all | solution.py:142
  168.3 6.8 %all-to-all-start.3 = ((bf16[64,2,8,512]{3,2,1,0:T(8,128)(2,1)}), bf16[64,2,8,512]{3,2,1,0:T(8,128)(2,1)}, u32[]{:S(2)}, u32[]{:S(2)}) async-start(bf16[64,2,8,512]{3,2,1,0:T(8,128)(2,1)} %bitcast.38), calls=%async_computation.4 | async-start | bytes 2097152 | tf_op jit(solution)/shard_map/all_to_all | solution.py:150
  175.1 3.8 copy_bitcast_fusion
  179.0 4.7 %copy.76 = bf16[2,512,1536]{1,2,0:T(8,128)(2,1)} copy(bf16[2,512,1536]{2,1,0:T(8,128)(2,1)} %copy_bitcast_fusion) | data formatting | bytes 6291456 | tf_op jit(solution)/shard_map/while | solution.py:146
  183.7 21.6 %while.34 = (s32[]{:T(128)}, bf16[2,512,512]{2,1,0:T(8,128)(2,1)}, bf16[2,512,1536]{1,2,0:T(8,128)(2,1)}, pred[2,512]{1,0:T(4,128)(4,1)S(1)}, s32[]{:T(128)}) while((s32[]{:T(128)}, bf16[2,512,512]{2,1,0:T(8,128)(2,1)}, bf16[2,512,1536]{1,2,0:T(8,128)(2,1)}, pred[2,512]{1,0:T(4,128)(4,1)S(1)}, s32[]{:T(128)}) %tuple.85), condition=%wide.region_11.12_spmd, body=%wide.region_8.11_spmd.sunk | while | flops 543425024 | bytes 18892868 | solution.py:146
  183.7 1.5 dynamic-slice_bitcast_fusion.4
  185.2 0.9 fusion.124
  186.1 4.7 %fusion.125 = (f32[4,512]{1,0:T(4,128)S(1)}, f32[4,512,512]{1,2,0:T(8,128)}) fusion(pred[512]{0:T(512)(128)(4,1)S(1)} %dynamic-slice_reduce_fusion.4, bf16[512,4,128]{0,2,1:T(8,128)(2,1)} %bitcast.166, bf16[512,4,128]{0,2,1:T(8,128)(2,1)S(1)} %bitcast.165), kind=kOutput, calls=%fused_computation.96.clone.1 | convolution fusion | flops 272630272 | bytes 5251584 | tf_op jit(solution)/shard_map/while/body/eval_jaxpr/sub | solution.py:33
  190.8 2.6 fusion.126
  193.6 0.8 constant_dynamic-update-slice_fusion.4
  194.5 1.5 dynamic-slice_bitcast_fusion.4
  196.0 0.9 fusion.124
  196.9 4.7 %fusion.125 = (f32[4,512]{1,0:T(4,128)S(1)}, f32[4,512,512]{1,2,0:T(8,128)}) fusion(pred[512]{0:T(512)(128)(4,1)S(1)} %dynamic-slice_reduce_fusion.4, bf16[512,4,128]{0,2,1:T(8,128)(2,1)} %bitcast.166, bf16[512,4,128]{0,2,1:T(8,128)(2,1)S(1)} %bitcast.165), kind=kOutput, calls=%fused_computation.96.clone.1 | convolution fusion | flops 272630272 | bytes 5251584 | tf_op jit(solution)/shard_map/while/body/eval_jaxpr/sub | solution.py:33
  201.6 2.6 fusion.126
  204.4 0.8 constant_dynamic-update-slice_fusion.4
  205.2 2.4 copy.78
  207.7 10.3 %all-to-all-start.2 = ((bf16[2,64,8,512]{3,2,0,1:T(8,128)(2,1)}), bf16[2,64,8,512]{3,2,0,1:T(8,128)(2,1)S(1)}, u32[]{:S(2)}, u32[]{:S(2)}) async-start(bf16[2,64,8,512]{3,2,0,1:T(8,128)(2,1)} %copy.78), calls=%async_computation.2 | async-start | bytes 2097152 | tf_op jit(solution)/shard_map/all_to_all | solution.py:148
  218.1 2.3 copy_bitcast_fusion.1
  220.4 25.6 %all-to-all-done.2 = bf16[2,64,8,512]{3,2,0,1:T(8,128)(2,1)S(1)} async-done(((bf16[2,64,8,512]{3,2,0,1:T(8,128)(2,1)}), bf16[2,64,8,512]{3,2,0,1:T(8,128)(2,1)S(1)}, u32[]{:S(2)}, u32[]{:S(2)}) %all-to-all-start.2) | async-done | bytes 1048608 | tf_op jit(solution)/shard_map/all_to_all | solution.py:148
  246.0 2.6 gather_fusion
  248.6 4.3 fusion.57
  253.1 60.3 %while.35 = (s32[]{:T(128)}, bf16[2,512,1536]{2,1,0:T(8,128)(2,1)}, bf16[2,512,1536]{1,2,0:T(8,128)(2,1)}, pred[2,512]{1,0:T(4,128)(4,1)S(1)}, bf16[2,512,512]{2,1,0:T(8,128)(2,1)}, /*index=5*/s32[]{:T(128)}) while((s32[]{:T(128)}, bf16[2,512,1536]{2,1,0:T(8,128)(2,1)}, bf16[2,512,1536]{1,2,0:T(8,128)(2,1)}, pred[2,512]{1,0:T(4,128)(4,1)S(1)}, ...), condition=%wide.region_18.19_spmd, body=%wide.region_14.18_spmd.sunk | while | flops 1368659456 | bytes 52463696 | solution.py:153
  253.1 1.5 dynamic-slice_bitcast_fusion.5
  254.8 3.7 fusion.138
  258.5 1.1 constant_dynamic-slice_fusion.2
  259.7 2.9 fusion.140
  262.7 7.8 %fusion.142 = bf16[4,128,512]{2,1,0:T(8,128)(2,1)S(1)} fusion(bf16[512,4,128]{0,2,1:T(8,128)(2,1)S(1)} %bitcast.162, f32[4,512,512]{1,2,0:T(8,128)} %fusion.140, f32[4,512,512]{1,2,0:T(8,128)} %get-tuple-element.302, f32[4,512]{1,0:T(4,128)S(1)} %get-tuple-element.303), kind=kOutput, calls=%fused_computation.44.clone.1 | convolution fusion | flops 276040192 | bytes 9445376 | tf_op jit(solution)/shard_map/while/body/eval_jaxpr/hqk,khd->qhd/dot_general | solution.py:69
  270.5 7.7 %fusion.141 = bf16[4,128,512]{2,1,0:T(8,128)(2,1)S(1)} fusion(bf16[512,4,128]{0,2,1:T(8,128)(2,1)S(1)} %bitcast.160, f32[4,512,512]{1,2,0:T(8,128)} %fusion.140, f32[4,512,512]{1,2,0:T(8,128)} %get-tuple-element.302, f32[4,512]{1,0:T(4,128)S(1)} %get-tuple-element.303), kind=kOutput, calls=%fused_computation.45.clone.1 | convolution fusion | flops 276040192 | bytes 9445376 | tf_op jit(solution)/shard_map/while/body/eval_jaxpr/hqk,qhd->khd/dot_general | solution.py:72
  278.2 3.1 fusion.139
  282.1 1.3 constant_dynamic-update-slice_fusion.5
  283.4 1.5 dynamic-slice_bitcast_fusion.5
  285.0 3.7 fusion.138
  288.7 1.1 constant_dynamic-slice_fusion.2
  290.0 2.7 fusion.140
  292.7 7.9 %fusion.142 = bf16[4,128,512]{2,1,0:T(8,128)(2,1)S(1)} fusion(bf16[512,4,128]{0,2,1:T(8,128)(2,1)S(1)} %bitcast.162, f32[4,512,512]{1,2,0:T(8,128)} %fusion.140, f32[4,512,512]{1,2,0:T(8,128)} %get-tuple-element.302, f32[4,512]{1,0:T(4,128)S(1)} %get-tuple-element.303), kind=kOutput, calls=%fused_computation.44.clone.1 | convolution fusion | flops 276040192 | bytes 9445376 | tf_op jit(solution)/shard_map/while/body/eval_jaxpr/hqk,khd->qhd/dot_general | solution.py:69
  300.6 7.6 %fusion.141 = bf16[4,128,512]{2,1,0:T(8,128)(2,1)S(1)} fusion(bf16[512,4,128]{0,2,1:T(8,128)(2,1)S(1)} %bitcast.160, f32[4,512,512]{1,2,0:T(8,128)} %fusion.140, f32[4,512,512]{1,2,0:T(8,128)} %get-tuple-element.302, f32[4,512]{1,0:T(4,128)S(1)} %get-tuple-element.303), kind=kOutput, calls=%fused_computation.45.clone.1 | convolution fusion | flops 276040192 | bytes 9445376 | tf_op jit(solution)/shard_map/while/body/eval_jaxpr/hqk,qhd->khd/dot_general | solution.py:72
  308.2 3.0 fusion.139
  312.1 1.3 constant_dynamic-update-slice_fusion.5
  313.4 2.3 copy.83
  315.7 79.5 %all_to_all.69 = bf16[2,64,8,1536]{3,2,0,1:T(8,128)(2,1)S(1)} all-to-all(bf16[2,64,8,1536]{3,2,0,1:T(8,128)(2,1)S(1)} %copy.83), channel_id=1, replica_groups=mesh['seq'=64,'tp'=4] {'seq'}, dimensions={1} | all-to-all | bytes 6291456 | tf_op jit(solution)/shard_map/all_to_all | solution.py:158
  395.2 3.0 gather_fusion.1
  398.1 1.7 broadcast_multiply_fusion
  400.2 1.3 fusion.51
  401.8 1.3 fusion.53
  403.4 3.3 add_add_fusion
  406.7 2.1 convert_element_type.87
  408.8 44.7 %reduce-scatter.5.cloned.1.call-done = f32[512,512]{1,0:T(8,128)} async-done(((f32[512,2048]{1,0:T(8,128)}), f32[512,512]{1,0:T(8,128)}) %reduce-scatter.5.cloned.1.call-update) | async-done | bytes 1048592 | tf_op jit(solution)/shard_map/reduce_scatter | solution.py:177
  (123 shorter events, 8.1 us)
Async XLA Ops:
  7.2 125.7 %copy-start = (bf16[512,2048]{1,0:T(8,128)(2,1)S(1)}, bf16[512,2048]{1,0:T(8,128)(2,1)}, u32[]{:S(2)}) copy-start(bf16[512,2048]{1,0:T(8,128)(2,1)} %param.18) | copy-start | bytes 6291460
  7.2 61.7 %all-gather.4.cloned.1.call-start = ((), (), s32[]{:S(2)}) async-start(), calls=%async_computation.7 | async-start | bytes 2621440 | tf_op jit(solution)/shard_map/all_gather | solution.py:100
  62.0 23.3 %all-to-all-start.1 = ((bf16[64,2,8]{2,1,0:T(2,128)(2,1)}), bf16[64,2,8]{2,1,0:T(2,128)(2,1)S(1)}, u32[]{:S(2)}, u32[]{:S(2)}) async-start(bf16[64,2,8]{2,1,0:T(2,128)(2,1)} %reshape.110), calls=%async_computation.1 | async-start | bytes 65536 | tf_op jit(solution)/shard_map/all_to_all | solution.py:143
  68.9 3.7 copy-start.2
  68.9 3.7 copy-start.7
  72.6 1.6 copy-start.4
  85.4 83.0 %all-to-all-start = ((bf16[64,2,8,1536]{3,2,1,0:T(8,128)(2,1)}), bf16[64,2,8,1536]{3,2,1,0:T(8,128)(2,1)}, u32[]{:S(2)}, u32[]{:S(2)}) async-start(bf16[64,2,8,1536]{3,2,1,0:T(8,128)(2,1)} %bitcast.169), calls=%async_computation | async-start | bytes 6291456 | tf_op jit(solution)/shard_map/all_to_all | solution.py:142
  95.8 37.0 %all-gather.6.cloned.1.call-start = ((), (), s32[]{:S(2)}) async-start(), calls=%async_computation.9 | async-start | bytes 2621440 | tf_op jit(solution)/shard_map/all_gather | solution.py:114
  168.3 39.4 %all-to-all-start.3 = ((bf16[64,2,8,512]{3,2,1,0:T(8,128)(2,1)}), bf16[64,2,8,512]{3,2,1,0:T(8,128)(2,1)}, u32[]{:S(2)}, u32[]{:S(2)}) async-start(bf16[64,2,8,512]{3,2,1,0:T(8,128)(2,1)} %bitcast.38), calls=%async_computation.4 | async-start | bytes 2097152 | tf_op jit(solution)/shard_map/all_to_all | solution.py:150
  207.7 38.3 %all-to-all-start.2 = ((bf16[2,64,8,512]{3,2,0,1:T(8,128)(2,1)}), bf16[2,64,8,512]{3,2,0,1:T(8,128)(2,1)S(1)}, u32[]{:S(2)}, u32[]{:S(2)}) async-start(bf16[2,64,8,512]{3,2,0,1:T(8,128)(2,1)} %copy.78), calls=%async_computation.2 | async-start | bytes 2097152 | tf_op jit(solution)/shard_map/all_to_all | solution.py:148
  218.0 188.7 %reduce-scatter.3.cloned.1.call-start = ((), (), s32[]{:S(2)}) async-start(), calls=%async_computation.8 | async-start | bytes 5242880 | tf_op jit(solution)/shard_map/reduce_scatter | solution.py:161
  252.9 200.6 %reduce-scatter.5.cloned.1.call-start = ((), (), s32[]{:S(2)}) async-start(), calls=%async_computation.10 | async-start | bytes 5242880 | tf_op jit(solution)/shard_map/reduce_scatter | solution.py:177
  398.1 2.1 copy-start.3
  400.2 1.6 copy-start.5
  401.8 1.6 copy-start.6
  403.4 50.1 %copy-start.1 = (bf16[512,2048]{1,0:T(8,128)(2,1)S(1)}, bf16[512,2048]{1,0:T(8,128)(2,1)}, u32[]{:S(2)}) copy-start(bf16[512,2048]{1,0:T(8,128)(2,1)} %param.18) | copy-start | bytes 6291460
Sparse Core Ops, SparseCore 0:
  9.8 37.1 all-gather.3
  98.5 34.2 all-gather.5
  253.0 46.4 reduce-scatter.2
  406.8 46.6 reduce-scatter.4
where the time goes:
time: 466 us; the launch traced here: 460 us
  waiting for transfers between devices  136 us (29%)
  blocking collectives  124 us (27%)
  matrix products  83.9 us (18%)
  local copies, waits for them, and re-layouts  56.7 us (12%)
  starting transfers between devices  35.3 us (8%)
  between operations  14.3 us (3%)
  other arithmetic  8.37 us (2%)
    all_to_all x1, blocking collectives, body(): lax.all_to_all(from_owners(grad_slots), 'seq', split_axis=1, concat_axis=...  79.5 us
    reduce_scatter x1, waiting for transfers between devices, body(): lax.psum_scatter(partial_grad, 'tp', scatter_dimension=1, tiled=True)  44.7 us
    all_gather x1, blocking collectives, entering(): everything = lax.all_gather(x, axis)  44.2 us
    all_gather x1, waiting for transfers between devices, body(): lax.all_gather(grad_out, 'tp', axis=1, tiled=True)  36 us
    all_to_all x1, waiting for transfers between devices, body(): lax.all_to_all(to_owners(packed_rows), 'seq', split_axis=0, concat_axis=2...  29.2 us
    all_to_all x1, waiting for transfers between devices, body(): lax.all_to_all(from_owners(mixed_slots), 'seq', split_axis=1, concat_axis...  25.6 us
    sub x4, matrix products, cluster_probs(): raised = jnp.exp(scores - row_top)  16.6 us
    dot_general x2, matrix products, attention_core(): jnp.einsum('hqk,khd->qhd', grad_scores, key_rows, preferred_element_type=...  15.7 us
  transfers between devices with their start and end apart: 8, of which 4 were waited for; matrix products, arithmetic and copies ran while one was open for 31% of the time, Pallas kernels for 0%

commit v1 on v0

--- a/solution.py
+++ b/solution.py
@@ -111,7 +111,15 @@
     )
     head_grads = (
         lax.dot_general(
-            lax.all_gather(grad_out, "tp", axis=1, tiled=True),
+            jnp.concatenate(
+                lax.all_to_all(
+                    jnp.stack([grad_out for _ in range(lax.axis_size("tp"))]),
+                    axis_name="tp",
+                    split_axis=0,
+                    concat_axis=0,
+                ),
+                axis=1,
+            ),
             w_out,
             (((1,), (1,)), ((), ())),
             preferred_element_type=jnp.float32,

time: 466 us -> 486 us (1.043)
  waiting for transfers between devices: 136 us -> 153 us
    all_to_all x1, waiting for transfers between devices: 29.2 us -> 66 us  [body(): lax.all_to_all(to_owners(packed_rows), 'seq', split_axis=0, concat_axis=2...]
    all_gather x1 -> x0, waiting for transfers between devices: 36 us -> none  [body(): lax.all_gather(grad_out, 'tp', axis=1, tiled=True)]
    all_to_all x0 -> x1, waiting for transfers between devices: none -> 9.25 us  [body(): lax.all_to_all(jnp.stack([grad_out for _ in range(lax.axis_size('tp'))]),...]
    all_to_all x1, waiting for transfers between devices: 0.01 us -> 8.04 us  [body(): lax.all_to_all(flags, 'seq', split_axis=0, concat_axis=2, tiled=True)]
  transfers between devices with their start and end apart: 8 -> 8, of which waited for: 4 -> 5; matrix products, arithmetic and copies ran while one was open for 31% -> 30% of each run, Pallas kernels for 0% -> 0%
where the time goes in v1:
time: 486 us; the launch traced here: 479 us
  waiting for transfers between devices  153 us (31%)
  blocking collectives  124 us (26%)
  matrix products  83.7 us (17%)
  local copies, waits for them, and re-layouts  59.5 us (12%)
  starting transfers between devices  35.7 us (7%)
  between operations  14.3 us (3%)
  other arithmetic  8.37 us (2%)
    all_to_all x1, blocking collectives, body(): lax.all_to_all(from_owners(grad_slots), 'seq', split_axis=1, concat_axis=...  79.5 us
    all_to_all x1, waiting for transfers between devices, body(): lax.all_to_all(to_owners(packed_rows), 'seq', split_axis=0, concat_axis=2...  66 us
    all_gather x1, blocking collectives, entering(): everything = lax.all_gather(x, axis)  44.2 us
    reduce_scatter x1, waiting for transfers between devices, body(): lax.psum_scatter(partial_grad, 'tp', scatter_dimension=1, tiled=True)  43 us
    all_to_all x1, waiting for transfers between devices, body(): lax.all_to_all(from_owners(mixed_slots), 'seq', split_axis=1, concat_axis...  25.6 us
    sub x4, matrix products, cluster_probs(): raised = jnp.exp(scores - row_top)  16.6 us
    dot_general x2, matrix products, attention_core(): jnp.einsum('hqk,khd->qhd', grad_scores, key_rows, preferred_element_type=...  15.7 us
    dot_general x2, matrix products, attention_core(): jnp.einsum('hqk,qhd->khd', grad_scores, query, preferred_element_type=jnp...  15.3 us
  transfers between devices with their start and end apart: 8, of which 5 were waited for; matrix products, arithmetic and copies ran while one was open for 30% of the time, Pallas kernels for 0%

profile of v1, /device:TPU:1, one launch (start us, length us, event | category | flops | bytes accessed | tf_op | source)
XLA Modules:
  0.0 479.4 jit_solution(12188896048590406434)
XLA Ops:
  9.0 44.2 %all-gather = s32[64,1,128]{2,1,0:T(1,128)S(1)} all-gather(s32[1,1,128]{2,1,0:T(1,128)S(1)} %slice_bitcast_fusion.1), channel_id=1, replica_groups=mesh['seq'=64,'tp'=4] {'seq'}, dimensions={0}, use_global_device_ids=true | all-gather | bytes 33280 | tf_op jit(solution)/shard_map/all_gather | solution.py:14
  53.3 2.6 while.36
  55.9 1.0 select_reduce_fusion
  57.5 3.8 scatter_custom_fusion.1
  62.0 6.4 %all-to-all-start.1 = ((bf16[64,2,8]{2,1,0:T(2,128)(2,1)}), bf16[64,2,8]{2,1,0:T(2,128)(2,1)S(1)}, u32[]{:S(2)}, u32[]{:S(2)}) async-start(bf16[64,2,8]{2,1,0:T(2,128)(2,1)} %reshape.118), calls=%async_computation.1 | async-start | bytes 65536 | tf_op jit(solution)/shard_map/all_to_all | solution.py:151
  68.5 1.3 copy.81
  69.7 8.0 %all-to-all-done.1 = bf16[64,2,8]{2,1,0:T(2,128)(2,1)S(1)} async-done(((bf16[64,2,8]{2,1,0:T(2,128)(2,1)}), bf16[64,2,8]{2,1,0:T(2,128)(2,1)S(1)}, u32[]{:S(2)}, u32[]{:S(2)}) %all-to-all-start.1) | async-done | bytes 2080 | tf_op jit(solution)/shard_map/all_to_all | solution.py:151
  77.8 1.5 stack.2
  79.3 4.8 all-to-all-start.3
  84.1 3.7 convolution_convert_fusion.1
  87.8 1.3 convolution_convert_fusion.2
  89.4 1.3 convolution_convert_fusion.3
  90.7 1.3 pad_maximum_fusion
  91.9 2.6 copy.75
  94.6 6.0 %scatter_custom_fusion = bf16[1024,1536]{1,0:T(8,128)(2,1)} fusion(s32[512]{0:T(512)S(1)} %bitcast.184, bf16[512,1536]{1,0:T(8,128)(2,1)} %copy.75, bf16[]{:T(256)} %constant.82.clone.1), kind=kCustom, calls=%fused_computation.59 | custom fusion | bytes 3146240 | tf_op jit(solution)/shard_map/scatter | solution.py:131
  100.6 9.3 %all-to-all-done.3 = bf16[4,512,512]{1,2,0:T(8,128)(2,1)} async-done(((bf16[4,512,512]{1,2,0:T(8,128)(2,1)}), bf16[4,512,512]{1,2,0:T(8,128)(2,1)}, u32[]{:S(2)}, u32[]{:S(2)}) %all-to-all-start.3) | async-done | bytes 2097184 | tf_op jit(solution)/shard_map/all_to_all | solution.py:115
  109.8 7.2 %all-to-all-start = ((bf16[64,2,8,1536]{3,2,1,0:T(8,128)(2,1)}), bf16[64,2,8,1536]{3,2,1,0:T(8,128)(2,1)}, u32[]{:S(2)}, u32[]{:S(2)}) async-start(bf16[64,2,8,1536]{3,2,1,0:T(8,128)(2,1)} %bitcast.172), calls=%async_computation | async-start | bytes 6291456 | tf_op jit(solution)/shard_map/all_to_all | solution.py:150
  117.2 2.9 fusion.49
  120.1 3.5 scatter_custom_fusion.2
  123.6 66.0 %all-to-all-done = bf16[64,2,8,1536]{3,2,1,0:T(8,128)(2,1)} async-done(((bf16[64,2,8,1536]{3,2,1,0:T(8,128)(2,1)}), bf16[64,2,8,1536]{3,2,1,0:T(8,128)(2,1)}, u32[]{:S(2)}, u32[]{:S(2)}) %all-to-all-start) | async-done | bytes 3145760 | tf_op jit(solution)/shard_map/all_to_all | solution.py:150
  189.6 6.7 %all-to-all-start.4 = ((bf16[64,2,8,512]{3,2,1,0:T(8,128)(2,1)}), bf16[64,2,8,512]{3,2,1,0:T(8,128)(2,1)}, u32[]{:S(2)}, u32[]{:S(2)}) async-start(bf16[64,2,8,512]{3,2,1,0:T(8,128)(2,1)} %bitcast.40), calls=%async_computation.5 | async-start | bytes 2097152 | tf_op jit(solution)/shard_map/all_to_all | solution.py:158
  196.3 3.8 copy_bitcast_fusion
  200.1 4.7 copy.78
  204.8 21.6 %while.34 = (s32[]{:T(128)}, bf16[2,512,512]{2,1,0:T(8,128)(2,1)}, bf16[2,512,1536]{1,2,0:T(8,128)(2,1)}, pred[2,512]{1,0:T(4,128)(4,1)S(1)}, s32[]{:T(128)}) while((s32[]{:T(128)}, bf16[2,512,512]{2,1,0:T(8,128)(2,1)}, bf16[2,512,1536]{1,2,0:T(8,128)(2,1)}, pred[2,512]{1,0:T(4,128)(4,1)S(1)}, s32[]{:T(128)}) %tuple.85), condition=%wide.region_11.12_spmd, body=%wide.region_8.11_spmd.sunk | while | flops 543425024 | bytes 18892868 | solution.py:154
  204.8 1.5 dynamic-slice_bitcast_fusion.4
  206.3 0.9 fusion.124
  207.2 4.7 fusion.125
  211.9 2.6 fusion.126
  215.6 1.5 dynamic-slice_bitcast_fusion.4
  217.1 0.9 fusion.124
  218.0 4.7 fusion.125
  222.7 2.6 fusion.126
  226.4 2.4 copy.80
  228.8 10.3 %all-to-all-start.2 = ((bf16[2,64,8,512]{3,2,0,1:T(8,128)(2,1)}), bf16[2,64,8,512]{3,2,0,1:T(8,128)(2,1)S(1)}, u32[]{:S(2)}, u32[]{:S(2)}) async-start(bf16[2,64,8,512]{3,2,0,1:T(8,128)(2,1)} %copy.80), calls=%async_computation.2 | async-start | bytes 2097152 | tf_op jit(solution)/shard_map/all_to_all | solution.py:156
  239.2 2.3 copy_bitcast_fusion.1
  241.5 25.6 %all-to-all-done.2 = bf16[2,64,8,512]{3,2,0,1:T(8,128)(2,1)S(1)} async-done(((bf16[2,64,8,512]{3,2,0,1:T(8,128)(2,1)}), bf16[2,64,8,512]{3,2,0,1:T(8,128)(2,1)S(1)}, u32[]{:S(2)}, u32[]{:S(2)}) %all-to-all-start.2) | async-done | bytes 1048608 | tf_op jit(solution)/shard_map/all_to_all | solution.py:156
  267.1 2.6 gather_fusion
  269.8 4.3 fusion.57
  274.3 60.0 %while.35 = (s32[]{:T(128)}, bf16[2,512,1536]{2,1,0:T(8,128)(2,1)}, bf16[2,512,1536]{1,2,0:T(8,128)(2,1)}, pred[2,512]{1,0:T(4,128)(4,1)S(1)}, bf16[2,512,512]{2,1,0:T(8,128)(2,1)}, /*index=5*/s32[]{:T(128)}) while((s32[]{:T(128)}, bf16[2,512,1536]{2,1,0:T(8,128)(2,1)}, bf16[2,512,1536]{1,2,0:T(8,128)(2,1)}, pred[2,512]{1,0:T(4,128)(4,1)S(1)}, ...), condition=%wide.region_18.19_spmd, body=%wide.region_14.18_spmd.sunk | while | flops 1368659456 | bytes 52463696 | solution.py:161
  274.3 1.5 dynamic-slice_bitcast_fusion.5
  275.9 3.7 fusion.138
  279.6 1.1 constant_dynamic-slice_fusion.2
  280.9 2.7 fusion.140
  283.6 7.8 %fusion.142 = bf16[4,128,512]{2,1,0:T(8,128)(2,1)S(1)} fusion(bf16[512,4,128]{0,2,1:T(8,128)(2,1)S(1)} %bitcast.165, f32[4,512,512]{1,2,0:T(8,128)} %fusion.140, f32[4,512,512]{1,2,0:T(8,128)} %get-tuple-element.302, f32[4,512]{1,0:T(4,128)S(1)} %get-tuple-element.303), kind=kOutput, calls=%fused_computation.44.clone.1 | convolution fusion | flops 276040192 | bytes 9445376 | tf_op jit(solution)/shard_map/while/body/eval_jaxpr/hqk,khd->qhd/dot_general | solution.py:69
  291.5 7.7 %fusion.141 = bf16[4,128,512]{2,1,0:T(8,128)(2,1)S(1)} fusion(bf16[512,4,128]{0,2,1:T(8,128)(2,1)S(1)} %bitcast.163, f32[4,512,512]{1,2,0:T(8,128)} %fusion.140, f32[4,512,512]{1,2,0:T(8,128)} %get-tuple-element.302, f32[4,512]{1,0:T(4,128)S(1)} %get-tuple-element.303), kind=kOutput, calls=%fused_computation.45.clone.1 | convolution fusion | flops 276040192 | bytes 9445376 | tf_op jit(solution)/shard_map/while/body/eval_jaxpr/hqk,qhd->khd/dot_general | solution.py:72
  299.1 3.0 fusion.139
  303.0 1.3 constant_dynamic-update-slice_fusion.5
  304.3 1.6 dynamic-slice_bitcast_fusion.5
  306.0 3.7 fusion.138
  309.6 1.1 constant_dynamic-slice_fusion.2
  310.9 2.7 fusion.140
  313.7 7.9 %fusion.142 = bf16[4,128,512]{2,1,0:T(8,128)(2,1)S(1)} fusion(bf16[512,4,128]{0,2,1:T(8,128)(2,1)S(1)} %bitcast.165, f32[4,512,512]{1,2,0:T(8,128)} %fusion.140, f32[4,512,512]{1,2,0:T(8,128)} %get-tuple-element.302, f32[4,512]{1,0:T(4,128)S(1)} %get-tuple-element.303), kind=kOutput, calls=%fused_computation.44.clone.1 | convolution fusion | flops 276040192 | bytes 9445376 | tf_op jit(solution)/shard_map/while/body/eval_jaxpr/hqk,khd->qhd/dot_general | solution.py:69
  321.6 7.6 %fusion.141 = bf16[4,128,512]{2,1,0:T(8,128)(2,1)S(1)} fusion(bf16[512,4,128]{0,2,1:T(8,128)(2,1)S(1)} %bitcast.163, f32[4,512,512]{1,2,0:T(8,128)} %fusion.140, f32[4,512,512]{1,2,0:T(8,128)} %get-tuple-element.302, f32[4,512]{1,0:T(4,128)S(1)} %get-tuple-element.303), kind=kOutput, calls=%fused_computation.45.clone.1 | convolution fusion | flops 276040192 | bytes 9445376 | tf_op jit(solution)/shard_map/while/body/eval_jaxpr/hqk,qhd->khd/dot_general | solution.py:72
  329.2 3.0 fusion.139
  333.0 1.3 constant_dynamic-update-slice_fusion.5
  334.3 2.3 copy.86
  336.7 79.5 %all_to_all.74 = bf16[2,64,8,1536]{3,2,0,1:T(8,128)(2,1)S(1)} all-to-all(bf16[2,64,8,1536]{3,2,0,1:T(8,128)(2,1)S(1)} %copy.86), channel_id=1, replica_groups=mesh['seq'=64,'tp'=4] {'seq'}, dimensions={1} | all-to-all | bytes 6291456 | tf_op jit(solution)/shard_map/all_to_all | solution.py:166
  416.1 3.0 gather_fusion.1
  419.1 1.7 broadcast_multiply_fusion
  421.1 1.3 fusion.51
  422.7 1.3 fusion.53
  424.3 3.3 add_add_fusion
  427.6 2.1 convert_element_type.87
  429.7 43.0 %reduce-scatter.5.cloned.1.call-done = f32[512,512]{1,0:T(8,128)} async-done(((f32[512,2048]{1,0:T(8,128)}), f32[512,512]{1,0:T(8,128)}) %reduce-scatter.5.cloned.1.call-update) | async-done | bytes 1048592 | tf_op jit(solution)/shard_map/reduce_scatter | solution.py:185
  (124 shorter events, 10.5 us)
Async XLA Ops:
  7.2 110.1 %copy-start = (bf16[512,2048]{1,0:T(8,128)(2,1)S(1)}, bf16[512,2048]{1,0:T(8,128)(2,1)}, u32[]{:S(2)}) copy-start(bf16[512,2048]{1,0:T(8,128)(2,1)} %param.18) | copy-start | bytes 6291460
  7.2 76.9 %all-gather.3.cloned.1.call-start = ((), (), s32[]{:S(2)}) async-start(), calls=%async_computation.8 | async-start | bytes 2621440 | tf_op jit(solution)/shard_map/all_gather | solution.py:100
  62.0 15.7 %all-to-all-start.1 = ((bf16[64,2,8]{2,1,0:T(2,128)(2,1)}), bf16[64,2,8]{2,1,0:T(2,128)(2,1)S(1)}, u32[]{:S(2)}, u32[]{:S(2)}) async-start(bf16[64,2,8]{2,1,0:T(2,128)(2,1)} %reshape.118), calls=%async_computation.1 | async-start | bytes 65536 | tf_op jit(solution)/shard_map/all_to_all | solution.py:151
  79.3 30.5 %all-to-all-start.3 = ((bf16[4,512,512]{1,2,0:T(8,128)(2,1)}), bf16[4,512,512]{1,2,0:T(8,128)(2,1)}, u32[]{:S(2)}, u32[]{:S(2)}) async-start(bf16[4,512,512]{1,2,0:T(8,128)(2,1)} %stack.2), calls=%async_computation.4 | async-start | bytes 4194304 | tf_op jit(solution)/shard_map/all_to_all | solution.py:115
  84.1 3.7 copy-start.2
  84.1 3.7 copy-start.7
  87.8 1.6 copy-start.4
  109.8 79.7 %all-to-all-start = ((bf16[64,2,8,1536]{3,2,1,0:T(8,128)(2,1)}), bf16[64,2,8,1536]{3,2,1,0:T(8,128)(2,1)}, u32[]{:S(2)}, u32[]{:S(2)}) async-start(bf16[64,2,8,1536]{3,2,1,0:T(8,128)(2,1)} %bitcast.172), calls=%async_computation | async-start | bytes 6291456 | tf_op jit(solution)/shard_map/all_to_all | solution.py:150
  189.6 39.3 %all-to-all-start.4 = ((bf16[64,2,8,512]{3,2,1,0:T(8,128)(2,1)}), bf16[64,2,8,512]{3,2,1,0:T(8,128)(2,1)}, u32[]{:S(2)}, u32[]{:S(2)}) async-start(bf16[64,2,8,512]{3,2,1,0:T(8,128)(2,1)} %bitcast.40), calls=%async_computation.5 | async-start | bytes 2097152 | tf_op jit(solution)/shard_map/all_to_all | solution.py:158
  228.8 38.3 %all-to-all-start.2 = ((bf16[2,64,8,512]{3,2,0,1:T(8,128)(2,1)}), bf16[2,64,8,512]{3,2,0,1:T(8,128)(2,1)S(1)}, u32[]{:S(2)}, u32[]{:S(2)}) async-start(bf16[2,64,8,512]{3,2,0,1:T(8,128)(2,1)} %copy.80), calls=%async_computation.2 | async-start | bytes 2097152 | tf_op jit(solution)/shard_map/all_to_all | solution.py:156
  239.1 188.5 %reduce-scatter.3.cloned.1.call-start = ((), (), s32[]{:S(2)}) async-start(), calls=%async_computation.9 | async-start | bytes 5242880 | tf_op jit(solution)/shard_map/reduce_scatter | solution.py:169
  274.0 198.6 %reduce-scatter.5.cloned.1.call-start = ((), (), s32[]{:S(2)}) async-start(), calls=%async_computation.10 | async-start | bytes 5242880 | tf_op jit(solution)/shard_map/reduce_scatter | solution.py:185
  419.1 2.1 copy-start.3
  421.1 1.6 copy-start.5
  422.7 1.6 copy-start.6
  424.3 48.4 %copy-start.1 = (bf16[512,2048]{1,0:T(8,128)(2,1)S(1)}, bf16[512,2048]{1,0:T(8,128)(2,1)}, u32[]{:S(2)}) copy-start(bf16[512,2048]{1,0:T(8,128)(2,1)} %param.18) | copy-start | bytes 6291460
Sparse Core Ops, SparseCore 0:
  9.8 37.1 all-gather.2
  274.2 44.6 reduce-scatter.2
  427.7 44.9 reduce-scatter.4
